TPU v7x, 32 devices: a whole 2x2x4 slice. The times are simulated.
32 devices in a mesh: groups: 2 (over x), ctx: 16 (over z, y, core).
Axes of the slice: x: 2, y: 2, z: 4, core: 2. Of those that a mesh axis runs over, the one named last changes fastest.
Arguments:
- queries: bfloat16 [4096, 4096], P(('groups', 'ctx')), parts along dimension 0, may hold values from -12 to 12
- keys: bfloat16 [4096, 512], P(('groups', 'ctx')), parts along dimension 0, may hold values from -9 to 9
- values: bfloat16 [4096, 512], P(('groups', 'ctx')), parts along dimension 0, may hold values from -6 to 6
- doc_lengths: int32 [32], P('groups'), parts along dimension 0, may hold values from 1 to 1024, 2048 in all
Outputs:
- attended: bfloat16 [4096, 4096], P(('groups', 'ctx')), parts along dimension 0
There are 2 independent parts, one for each index of `groups`. A program takes and returns all parts, laid end to end along the dimension named above; each array names one. Nothing has to cross between parts.
Inputs may be any that keep to these rules, and one draw needn't show every extreme that they name: `doc_lengths`: the lengths sum to 2048, and the longest document has exactly 1024 tokens.
All inputs are finite; a program needn't handle non-finite values.
Results may differ from a plain program's by a relative error of at most 0.003.
Values may be sent and summed in bfloat16 or wider, within the bound.
A program may use at most 128 MiB of HBM per device.

v0:
```python
import functools
import math

import jax
import jax.numpy as jnp
from jax import lax
from jax.experimental import pallas as pl
from jax.experimental.pallas import tpu as pltpu
from jax.sharding import PartitionSpec as P

HEADS = 32
KV_HEADS = 4
HEAD_DIM = 128
GROUP = HEADS // KV_HEADS
HEADS_PER_STEP = 2
FILLER = -1e30
EARLY = 2
ORDER = (
    ("own", 0),
    ("own", 1),
    ("near", 0),
    ("own", 2),
    ("near", 1),
    ("own", 3),
    ("far", 0),
    ("near", 2),
    ("far", 1),
    ("last", 0),
    ("near", 3),
    ("far", 2),
    ("last", 1),
    ("attend", 0),
    ("far", 3),
    ("last", 2),
    ("attend", 1),
    ("last", 3),
    ("attend", 2),
    ("attend", 3),
)


def kernel(
    n, level, q_hbm, k_hbm, v_hbm, len_ref, out_ref,
    q_buf, kv_buf, bias, own_sem, q_sem, send_sem, recv_sem,
):
    rows = q_hbm.shape[0]
    reach = n // 2
    far = reach // level
    planes = n // level
    width = (reach + 1) * rows
    me = lax.axis_index("ctx")
    z, r = me // level, me % level
    core = r + 1 - 2 * (r % 2)
    side = (r + 2) % level
    side_core = core + side - r

    def slot(d, lane):
        return (far - d) * level + lane

    def part(j, s):
        return kv_buf.at[j, :, pl.ds(pl.multiple_of(s * rows, rows), rows), :]

    def move(j, s, s_there, kind, device):
        return pltpu.make_async_remote_copy(
            src_ref=part(j, s), dst_ref=part(j, s_there),
            send_sem=send_sem.at[j, s, kind], recv_sem=recv_sem.at[j, s_there],
            device_id={"ctx": device}, device_id_type=pl.DeviceIdType.MESH,
        )

    def need(d, source, target):
        distance = d * level + target - source
        return (distance >= 0) & (distance <= reach)

    def there(d):
        return z >= d

    sent = []

    def send(condition, j, s, s_there, kind, device):
        @pl.when(condition)
        def _():
            move(j, s, s_there, kind, device).start()

        sent.append((condition, j, s, s_there, kind, device))

    def arrived(condition, j, s):
        @pl.when(condition)
        def _():
            move(j, s, s, 0, me - r + core).wait_recv()

    own = slot(0, r)
    own_copies = []
    for j in range(KV_HEADS):
        for t, ref in enumerate((k_hbm, v_hbm)):
            own_copies.append(pltpu.make_async_copy(
                ref.at[:, pl.ds(j * HEAD_DIM, HEAD_DIM)],
                kv_buf.at[j, t, pl.ds(pl.multiple_of(own * rows, rows), rows), :],
                own_sem.at[j, t],
            ))
            own_copies[-1].start()
    q_copy = pltpu.make_async_copy(q_hbm, q_buf, q_sem)
    q_copy.start()

    barrier = pltpu.get_barrier_semaphore()

    def greet(device):
        pl.semaphore_signal(
            barrier, inc=1, device_id={"ctx": device}, device_id_type=pl.DeviceIdType.MESH
        )

    greet(me - r + core)
    if level > 2:
        greet(me - r + side)

    @pl.when(z > 0)
    def _():
        greet(me - level)

    @pl.when(z < planes - 1)
    def _():
        greet(me + level)

    pl.semaphore_wait(
        barrier,
        (2 if level > 2 else 1) + (z > 0).astype(jnp.int32) + (z < planes - 1).astype(jnp.int32),
    )

    def spread(d, j):
        s = slot(d, r)
        if d < far:
            send(there(d) & (z < planes - 1), j, s, slot(d + 1, r), 0, me + level)
        if level > 2:
            send(
                there(d) & (need(d, r, side) | need(d, r, side_core)),
                j, s, s, 1, me - r + side,
            )
        send(there(d) & need(d, r, core), j, s, s, 2, me - r + core)

    def from_plane(j, d):
        arrived(there(d), j, slot(d, r))
        spread(d, j)

    def from_side(j, d):
        if level > 2:
            s = slot(d, side)
            arrived(there(d) & (need(d, side, r) | need(d, side, core)), j, s)
            send(there(d) & need(d, side, core), j, s, s, 2, me - r + core)

    def from_core(j):
        for d in range(far + 1):
            arrived(there(d) & need(d, core, r), j, slot(d, core))
            if level > 2:
                arrived(there(d) & need(d, side_core, r), j, slot(d, side_core))

    unit = (
        lax.broadcasted_iota(jnp.int32, (rows, rows), 0)
        == lax.broadcasted_iota(jnp.int32, (rows, rows), 1)
    ).astype(bias.dtype)
    factor = math.log2(math.e) / math.sqrt(HEAD_DIM)

    def attend(j):
        window = pl.ds(pl.multiple_of(r * rows, rows), width)

        @pl.loop(0, GROUP // HEADS_PER_STEP, unroll=True)
        def _(step):
            first = (j * GROUP + step * HEADS_PER_STEP) * HEAD_DIM
            columns = [
                pl.ds(pl.multiple_of(first + h * HEAD_DIM, HEAD_DIM), HEAD_DIM)
                for h in range(HEADS_PER_STEP)
            ]
            key_block = jnp.concatenate([kv_buf[j, 0, window, :], bias[...]], axis=1)
            value_block = kv_buf[j, 1, window, :]
            wide = jnp.concatenate([value_block, jnp.ones_like(value_block)], axis=1)
            block = jnp.concatenate(
                [jnp.concatenate([q_buf[:, c], unit], axis=1) for c in columns], axis=0
            )
            scores = lax.dot_general(
                block, key_block, (((1,), (1,)), ((), ())), preferred_element_type=jnp.float32
            )
            top = jnp.max(scores, axis=1, keepdims=True)
            weights = jnp.exp2((scores - top) * factor).astype(jnp.bfloat16)
            total = jnp.dot(weights, wide, preferred_element_type=jnp.float32)
            result = (total[:, :HEAD_DIM] / total[:, HEAD_DIM:]).astype(out_ref.dtype)
            for h, c in enumerate(columns):
                out_ref[:, c] = result[h * rows:(h + 1) * rows]

    def stage(kind, j):
        if kind == "own":
            own_copies[2 * j].wait()
            own_copies[2 * j + 1].wait()
            spread(0, j)
        elif kind == "near":
            from_plane(j, 1)
        elif kind == "far":
            from_side(j, 0)
            for d in range(2, far + 1):
                from_plane(j, d)
                from_side(j, d - 1)
        elif kind == "last":
            from_side(j, far)
        else:
            from_core(j)
            attend(j)

    for kind, j in ORDER[:EARLY]:
        stage(kind, j)

    for d in range(1, far + 1):
        @pl.when(z < d)
        def _():
            @pl.loop(0, KV_HEADS)
            def _(j):
                kv_buf[j, :, pl.ds(slot(d, 0) * rows, level * rows), :] = jnp.zeros(
                    (2, level * rows, HEAD_DIM), kv_buf.dtype
                )

    position = me * rows + lax.broadcasted_iota(jnp.int32, (width, rows), 1)
    key_position = (me - reach) * rows + lax.broadcasted_iota(jnp.int32, (width, rows), 0)
    start = jnp.zeros((width, rows), jnp.int32)
    end = jnp.int32(0)
    for k in range(len_ref.shape[0]):
        end = end + len_ref[k]
        start = jnp.where(end <= position, end, start)
    visible = (key_position >= start) & (key_position <= position)
    bias[...] = jnp.where(visible, 0.0, FILLER).astype(bias.dtype)

    q_copy.wait()
    for kind, j in ORDER[EARLY:]:
        stage(kind, j)

    for condition, *rest in sent:
        @pl.when(condition)
        def _():
            move(*rest).wait_send()


def solution(mesh):
    n = mesh.shape["ctx"]
    level = max(2, 8 // mesh.shape["groups"])

    def local(queries, keys, values, doc_lengths):
        rows = queries.shape[0]
        reach = n // 2
        slots = reach + level
        return pl.pallas_call(
            functools.partial(kernel, n, level),
            out_shape=jax.ShapeDtypeStruct(queries.shape, queries.dtype),
            in_specs=[pl.BlockSpec(memory_space=pltpu.HBM)] * 3
            + [pl.BlockSpec(memory_space=pltpu.SMEM)],
            out_specs=pl.BlockSpec(memory_space=pltpu.VMEM),
            scratch_shapes=[
                pltpu.VMEM(queries.shape, queries.dtype),
                pltpu.VMEM((KV_HEADS, 2, slots * rows, HEAD_DIM), keys.dtype),
                pltpu.VMEM(((reach + 1) * rows, rows), keys.dtype),
                pltpu.SemaphoreType.DMA((KV_HEADS, 2)),
                pltpu.SemaphoreType.DMA,
                pltpu.SemaphoreType.DMA((KV_HEADS, slots, 3)),
                pltpu.SemaphoreType.DMA((KV_HEADS, slots)),
            ],
            compiler_params=pltpu.CompilerParams(collective_id=0, has_side_effects=True,
                                                 vmem_limit_bytes=min(60 << 20, (3 * n // 2) << 20)),
        )(*(pltpu.with_memory_space_constraint(x, pltpu.HBM) for x in (queries, keys, values)), doc_lengths)

    spec = P(("groups", "ctx"), None)
    return jax.shard_map(
        local, mesh=mesh, in_specs=(spec, spec, spec, P("groups")), out_specs=spec, check_vma=False
    )
```

profile of v0, /device:TPU:18, one launch (start us, length us, event | category | flops | bytes accessed | tf_op | source)
XLA Modules:
  0.0 27.6 jit_solution(6145286220482084863)
XLA Ops:
  0.0 0.0 copy-start
  0.0 0.7 %copy-done = s32[16]{0:T(128)S(1)} copy-done((s32[16]{0:T(128)S(1)}, s32[16]{0:T(128)}, u32[]{:S(2)}) %copy-start) | copy-done | bytes 88
  0.7 25.9 %shard_map.46 = bf16[128,4096]{1,0:T(8,128)(2,1)S(1)} custom-call(bf16[128,4096]{1,0:T(8,128)(2,1)} %q_hbm.1, bf16[128,512]{1,0:T(8,128)(2,1)} %k_hbm.1, bf16[128,512]{1,0:T(8,128)(2,1)} %v_hbm.1, s32[16]{0:T(128)S(1)} %copy-done), custom_call_target="tpu_custom_call" | custom-call | tf_op jit(solution)/shard_map/pallas_call | solution.py:245
  26.6 1.0 %copy.6 = bf16[128,4096]{1,0:T(8,128)(2,1)} copy(bf16[128,4096]{1,0:T(8,128)(2,1)S(1)} %shard_map.46) | data formatting | bytes 2097152
Async XLA Ops:
  0.0 0.7 %copy-start = (s32[16]{0:T(128)S(1)}, s32[16]{0:T(128)}, u32[]{:S(2)}) copy-start(s32[16]{0:T(128)} %len_ref.1) | copy-start | bytes 196
where the time goes:
time: 27.7 us; the launch traced here: 27.6 us
  Pallas kernels  25.9 us (94%)
  local copies, waits for them, and re-layouts  1.63 us (6%)
    pallas_call x1, Pallas kernels, local(): pl.pallas_call(functools.partial(kernel, n, level), out_shape=jax.ShapeDt...  25.9 us
    unnamed x3, local copies, waits for them, and re-layouts  1.63 us

commit v1 on v0

v1 whole, which is shorter than its diff:
```python
import functools
import math

import jax
import jax.numpy as jnp
from jax import lax
from jax.experimental import pallas as pl
from jax.experimental.pallas import tpu as pltpu
from jax.sharding import PartitionSpec as P

HEADS = 32
KV_HEADS = 4
HEAD_DIM = 128
GROUP = HEADS // KV_HEADS
FILLER = -1e30
MAIN_HEADS = 2
TAIL_HEADS = 4
ORDER = (
    ("relay", 0),
    ("relay", 1),
    ("main", (0,)),
    ("relay", 2),
    ("main", (1,)),
    ("relay", 3),
    ("main", (2,)),
    ("last", 0),
    ("main", (3,)),
    ("last", 1),
    ("tail", (0,)),
    ("last", 2),
    ("tail", (1,)),
    ("last", 3),
    ("tail", (2,)),
    ("tail", (3,)),
)


def kernel(
    n, level, q_hbm, k_hbm, v_hbm, len_hbm, out_ref,
    q_buf, kv_buf, bias, len_buf, part_sum, part_top,
    own_sem, q_sem, len_sem, send_sem, recv_sem,
):
    rows = q_hbm.shape[0]
    reach = n // 2
    far = reach // level
    planes = n // level
    width = (reach + 1) * rows
    me = lax.axis_index("ctx")
    z, r = me // level, me % level
    core = r + 1 - 2 * (r % 2)
    side = (r + 2) % level
    side_core = core + side - r

    def slot(d, lane):
        return (far - d) * level + lane

    def part(j, s):
        return kv_buf.at[j, :, pl.ds(pl.multiple_of(s * rows, rows), rows), :]

    def move(j, s, s_there, kind, device):
        return pltpu.make_async_remote_copy(
            src_ref=part(j, s), dst_ref=part(j, s_there),
            send_sem=send_sem.at[j, s, kind], recv_sem=recv_sem.at[j, s_there],
            device_id={"ctx": device}, device_id_type=pl.DeviceIdType.MESH,
        )

    def need(d, source, target):
        distance = d * level + target - source
        return (distance >= 0) & (distance <= reach)

    def there(d):
        return z >= d

    sent = []

    def send(condition, j, s, s_there, kind, device):
        @pl.when(condition)
        def _():
            move(j, s, s_there, kind, device).start()

        sent.append((condition, j, s, s_there, kind, device))

    def arrived(condition, j, s):
        @pl.when(condition)
        def _():
            move(j, s, s, 0, me - r + core).wait_recv()

    barrier = pltpu.get_barrier_semaphore()

    def greet(device):
        pl.semaphore_signal(
            barrier, inc=1, device_id={"ctx": device}, device_id_type=pl.DeviceIdType.MESH
        )

    greet(me - r + core)
    if level > 2:
        greet(me - r + side)

    @pl.when(z > 0)
    def _():
        greet(me - level)

    @pl.when(z < planes - 1)
    def _():
        greet(me + level)

    own = slot(0, r)
    own_copies = []
    for j in range(KV_HEADS):
        for t, ref in enumerate((k_hbm, v_hbm)):
            own_copies.append(pltpu.make_async_copy(
                ref.at[:, pl.ds(j * HEAD_DIM, HEAD_DIM)],
                kv_buf.at[j, t, pl.ds(pl.multiple_of(own * rows, rows), rows), :],
                own_sem.at[j, t],
            ))
            own_copies[-1].start()
    q_copy = pltpu.make_async_copy(q_hbm, q_buf, q_sem)
    q_copy.start()
    len_copy = pltpu.make_async_copy(len_hbm, len_buf, len_sem)
    len_copy.start()

    pl.semaphore_wait(
        barrier,
        (2 if level > 2 else 1) + (z > 0).astype(jnp.int32) + (z < planes - 1).astype(jnp.int32),
    )

    def spread(d, j):
        s = slot(d, r)
        if d < far:
            send(there(d) & (z < planes - 1), j, s, slot(d + 1, r), 0, me + level)
        if level > 2:
            send(
                there(d) & (need(d, r, side) | need(d, r, side_core)),
                j, s, s, 1, me - r + side,
            )
        send(there(d) & need(d, r, core), j, s, s, 2, me - r + core)

    def from_plane(j, d):
        arrived(there(d), j, slot(d, r))
        spread(d, j)

    def from_side(j, d):
        if level > 2:
            s = slot(d, side)
            wanted = there(d) & (need(d, side, r) | need(d, side, core))
            arrived(wanted, j, s)
            send(there(d) & need(d, side, core), j, s, s, 2, me - r + core)

    def from_core(j, d):
        arrived(there(d) & need(d, core, r), j, slot(d, core))

    def from_core_side(j, d):
        if level > 2:
            arrived(there(d) & need(d, side_core, r), j, slot(d, side_core))

    unit = (
        lax.broadcasted_iota(jnp.int32, (rows, rows), 0)
        == lax.broadcasted_iota(jnp.int32, (rows, rows), 1)
    ).astype(bias.dtype)
    factor = math.log2(math.e) / math.sqrt(HEAD_DIM)

    def blocks(pieces):
        return [pl.ds(pl.multiple_of(first * rows, rows), count * rows) for first, count in pieces]

    main_pieces = [(level, reach + 1 - level)]
    tail_pieces = [(0, level)]

    def operands(j, pieces):
        places = blocks([(r + first, count) for first, count in pieces])
        keys = jnp.concatenate([kv_buf[j, 0, p, :] for p in places], axis=0)
        mask = jnp.concatenate([bias[p, :] for p in blocks(pieces)], axis=0)
        value_block = jnp.concatenate([kv_buf[j, 1, p, :] for p in places], axis=0)
        wide = jnp.concatenate([value_block, jnp.ones_like(value_block)], axis=1)
        return jnp.concatenate([keys, mask], axis=1), wide

    def columns(j, step, heads):
        first = j * GROUP + step * heads
        return [pl.ds((first + h) * HEAD_DIM, HEAD_DIM) for h in range(heads)]

    def pipelined(chosen, pieces, heads, ahead, finish):
        tasks = [(j, step) for j in chosen for step in range(GROUP // heads)]
        queue = []

        def begin(j, step):
            block = jnp.concatenate(
                [jnp.concatenate([q_buf[:, c], unit], axis=1) for c in columns(j, step, heads)],
                axis=0,
            )
            key_block, wide = operands(j, pieces)
            queue.append((lax.dot_general(
                block, key_block, (((1,), (1,)), ((), ())), preferred_element_type=jnp.float32
            ), wide))

        for task in tasks[:ahead]:
            begin(*task)
        for i, (j, step) in enumerate(tasks):
            if i + ahead < len(tasks):
                begin(*tasks[i + ahead])
            finish(j, step, heads, *queue.pop(0))

    def main_finish(j, step, heads, scores, wide):
        part = pl.ds(step * heads * rows, heads * rows)
        top = jnp.max(scores, axis=1, keepdims=True)
        weights = jnp.exp2((scores - top) * factor).astype(jnp.bfloat16)
        part_sum[j, part, :] = jnp.dot(weights, wide, preferred_element_type=jnp.float32)
        part_top[j, part, :] = jnp.broadcast_to(top, (heads * rows, HEAD_DIM))

    def tail_finish(j, step, heads, scores, wide):
        part = pl.ds(step * heads * rows, heads * rows)
        before = part_top[j, part, :]
        top = jnp.maximum(before, jnp.max(scores, axis=1, keepdims=True))
        weights = jnp.exp2((scores - top[:, :1]) * factor).astype(jnp.bfloat16)
        kept = jnp.exp2((before - top) * factor)
        total = jnp.dot(weights, wide, preferred_element_type=jnp.float32)
        summed = total[:, :HEAD_DIM] + kept * part_sum[j, part, :HEAD_DIM]
        weight = total[:, HEAD_DIM:] + kept * part_sum[j, part, HEAD_DIM:]
        result = (summed / weight).astype(out_ref.dtype)
        for h, c in enumerate(columns(j, step, heads)):
            out_ref[:, c] = result[h * rows:(h + 1) * rows]

    def stage(kind, what):
        if kind == "relay":
            from_side(what, far - 1)
            from_plane(what, far)
        elif kind == "last":
            from_side(what, far)
        elif kind == "main":
            for j in what:
                for d in range(far):
                    from_core(j, d)
                    from_core_side(j, d)
            pipelined(what, main_pieces, MAIN_HEADS, 2, main_finish)
        else:
            for j in what:
                from_core(j, far)
                from_core_side(j, far)
            pipelined(what, tail_pieces, TAIL_HEADS, 1, tail_finish)

    for j in range(KV_HEADS):
        own_copies[2 * j].wait()
        own_copies[2 * j + 1].wait()
        spread(0, j)

    for d in range(1, far + 1):
        @pl.when(z < d)
        def _():
            @pl.loop(0, KV_HEADS)
            def _(j):
                kv_buf[j, :, pl.ds(slot(d, 0) * rows, level * rows), :] = jnp.zeros(
                    (2, level * rows, HEAD_DIM), kv_buf.dtype
                )

    len_copy.wait()
    position = me * rows + lax.broadcasted_iota(jnp.int32, (1, rows), 1)
    start = jnp.zeros((1, rows), jnp.int32)
    end = jnp.int32(0)
    for k in range(len_buf.shape[0]):
        end = end + len_buf[k]
        start = jnp.where(end <= position, end, start)
    key_position = (me - reach) * rows + lax.broadcasted_iota(jnp.int32, (width, rows), 0)
    visible = (key_position >= start) & (key_position <= position)
    bias[...] = jnp.where(visible, 0.0, FILLER).astype(bias.dtype)

    for d in range(1, far):
        for j in range(KV_HEADS):
            from_plane(j, d)
            from_side(j, d - 1)
    q_copy.wait()
    for kind, what in ORDER:
        stage(kind, what)

    for condition, *rest in sent:
        @pl.when(condition)
        def _():
            move(*rest).wait_send()


def solution(mesh):
    n = mesh.shape["ctx"]
    level = max(2, 8 // mesh.shape["groups"])

    def local(queries, keys, values, doc_lengths):
        rows = queries.shape[0]
        reach = n // 2
        slots = reach + level
        return pl.pallas_call(
            functools.partial(kernel, n, level),
            out_shape=jax.ShapeDtypeStruct(queries.shape, queries.dtype),
            in_specs=[pl.BlockSpec(memory_space=pltpu.HBM)] * 4,
            out_specs=pl.BlockSpec(memory_space=pltpu.VMEM),
            scratch_shapes=[
                pltpu.VMEM(queries.shape, queries.dtype),
                pltpu.VMEM((KV_HEADS, 2, slots * rows, HEAD_DIM), keys.dtype),
                pltpu.VMEM(((reach + 1) * rows, rows), keys.dtype),
                pltpu.SMEM(doc_lengths.shape, doc_lengths.dtype),
                pltpu.VMEM((KV_HEADS, GROUP * rows, 2 * HEAD_DIM), jnp.float32),
                pltpu.VMEM((KV_HEADS, GROUP * rows, HEAD_DIM), jnp.float32),
                pltpu.SemaphoreType.DMA((KV_HEADS, 2)),
                pltpu.SemaphoreType.DMA,
                pltpu.SemaphoreType.DMA,
                pltpu.SemaphoreType.DMA((KV_HEADS, slots, 3)),
                pltpu.SemaphoreType.DMA((KV_HEADS, slots)),
            ],
            compiler_params=pltpu.CompilerParams(collective_id=0, has_side_effects=True,
                                                 vmem_limit_bytes=min(60 << 20, (3 * n // 2 + 8) << 20)),
        )(*(
            pltpu.with_memory_space_constraint(x, pltpu.HBM)
            for x in (queries, keys, values, doc_lengths)
        ))

    spec = P(("groups", "ctx"), None)
    return jax.shard_map(
        local, mesh=mesh, in_specs=(spec, spec, spec, P("groups")), out_specs=spec, check_vma=False
    )
```

time: 27.7 us -> 25.2 us (0.910)
  the two profiles are of different devices: /device:TPU:18 before, /device:TPU:25 now
where the time goes in v1:
time: 25.2 us; the launch traced here: 25.1 us
  Pallas kernels  24.1 us (96%)
  local copies, waits for them, and re-layouts  0.97 us (4%)
    pallas_call x1, Pallas kernels, local(): pl.pallas_call(functools.partial(kernel, n, level), out_shape=jax.ShapeDt...  24.1 us
    unnamed x1, local copies, waits for them, and re-layouts  0.97 us

profile of v1, /device:TPU:25, one launch (start us, length us, event | category | flops | bytes accessed | tf_op | source)
XLA Modules:
  0.0 25.1 jit_solution(10122357421372799385)
XLA Ops:
  0.0 24.1 %shard_map.46 = bf16[128,4096]{1,0:T(8,128)(2,1)S(1)} custom-call(bf16[128,4096]{1,0:T(8,128)(2,1)} %q_hbm.1, bf16[128,512]{1,0:T(8,128)(2,1)} %k_hbm.1, bf16[128,512]{1,0:T(8,128)(2,1)} %v_hbm.1, s32[16]{0:T(128)} %len_hbm.1), custom_call_target="tpu_custom_call" | custom-call | tf_op jit(solution)/shard_map/pallas_call | solution.py:286
  24.1 1.0 %copy.6 = bf16[128,4096]{1,0:T(8,128)(2,1)} copy(bf16[128,4096]{1,0:T(8,128)(2,1)S(1)} %shard_map.46) | data formatting | bytes 2097152

commit v2 on v1

--- a/solution.py
+++ b/solution.py
@@ -13,25 +13,38 @@
 HEAD_DIM = 128
 GROUP = HEADS // KV_HEADS
 FILLER = -1e30
+BY_PLANE = 1
 MAIN_HEADS = 2
-TAIL_HEADS = 4
+MAIN_AHEAD = 2
+MIDDLE_HEADS = 2
+MIDDLE_AHEAD = 0
+TAIL_HEADS = 2
+TAIL_AHEAD = 0
 ORDER = (
+    ("near", 0),
+    ("near", 1),
+    ("main", 0),
+    ("near", 2),
+    ("main", 1),
+    ("near", 3),
+    ("main", 2),
     ("relay", 0),
+    ("main", 3),
     ("relay", 1),
-    ("main", (0,)),
+    ("middle", 0),
     ("relay", 2),
-    ("main", (1,)),
+    ("middle", 1),
     ("relay", 3),
-    ("main", (2,)),
+    ("middle", 2),
     ("last", 0),
-    ("main", (3,)),
+    ("middle", 3),
     ("last", 1),
-    ("tail", (0,)),
+    ("last", 3),
+    ("tail", 0),
     ("last", 2),
-    ("tail", (1,)),
-    ("last", 3),
-    ("tail", (2,)),
-    ("tail", (3,)),
+    ("tail", 1),
+    ("tail", 3),
+    ("tail", 2),
 )
 
 
@@ -44,7 +57,6 @@
     reach = n // 2
     far = reach // level
     planes = n // level
-    width = (reach + 1) * rows
     me = lax.axis_index("ctx")
     z, r = me // level, me % level
     core = r + 1 - 2 * (r % 2)
@@ -124,11 +136,14 @@
         (2 if level > 2 else 1) + (z > 0).astype(jnp.int32) + (z < planes - 1).astype(jnp.int32),
     )
 
+    def by_plane(j):
+        return level > 2 and j >= KV_HEADS - BY_PLANE
+
     def spread(d, j):
         s = slot(d, r)
         if d < far:
             send(there(d) & (z < planes - 1), j, s, slot(d + 1, r), 0, me + level)
-        if level > 2:
+        if level > 2 and not (d == far and by_plane(j)):
             send(
                 there(d) & (need(d, r, side) | need(d, r, side_core)),
                 j, s, s, 1, me - r + side,
@@ -143,7 +158,12 @@
         if level > 2:
             s = slot(d, side)
             wanted = there(d) & (need(d, side, r) | need(d, side, core))
+            if by_plane(j) and d == far:
+                wanted = there(d) & (r < level // 2)
             arrived(wanted, j, s)
+            if by_plane(j) and d == far - 1:
+                climbs = there(d) & (r < level // 2) & (z < planes - 1)
+                send(climbs, j, s, slot(far, side), 0, me + level)
             send(there(d) & need(d, side, core), j, s, s, 2, me - r + core)
 
     def from_core(j, d):
@@ -162,13 +182,31 @@
     def blocks(pieces):
         return [pl.ds(pl.multiple_of(first * rows, rows), count * rows) for first, count in pieces]
 
-    main_pieces = [(level, reach + 1 - level)]
-    tail_pieces = [(0, level)]
+    if level > 2:
+        upper = r // 2
+        third = (r == 2).astype(jnp.int32)
+        first = (r == 0).astype(jnp.int32)
+        main_pieces = [
+            (4 + upper * (r + 1), 4 + upper * (r + 1) - r, 2),
+            (8 + upper * (r - 1), 8 + upper * (r - 1) - r, 1),
+            (8 + r, 8 + first, 1),
+        ]
+        middle_pieces = [
+            (r + 2 * upper, 2 * upper, 1),
+            (7 - third - 6 * first, 9 - 8 * first, 1),
+            (6 - third, 6 - third - r, 2),
+        ]
+        tail_pieces = [(2 + r // 3, 2 + r // 3 - r, 2)]
+    else:
+        main_pieces = [(r + level, level, reach + 1 - level)]
+        tail_pieces = [(r, 0, level)]
 
     def operands(j, pieces):
-        places = blocks([(r + first, count) for first, count in pieces])
+        places = blocks([(place, count) for place, _, count in pieces])
         keys = jnp.concatenate([kv_buf[j, 0, p, :] for p in places], axis=0)
-        mask = jnp.concatenate([bias[p, :] for p in blocks(pieces)], axis=0)
+        mask = jnp.concatenate(
+            [bias[p, :] for p in blocks([(distance, count) for _, distance, count in pieces])], axis=0
+        )
         value_block = jnp.concatenate([kv_buf[j, 1, p, :] for p in places], axis=0)
         wide = jnp.concatenate([value_block, jnp.ones_like(value_block)], axis=1)
         return jnp.concatenate([keys, mask], axis=1), wide
@@ -205,36 +243,54 @@
         part_sum[j, part, :] = jnp.dot(weights, wide, preferred_element_type=jnp.float32)
         part_top[j, part, :] = jnp.broadcast_to(top, (heads * rows, HEAD_DIM))
 
-    def tail_finish(j, step, heads, scores, wide):
-        part = pl.ds(step * heads * rows, heads * rows)
+    def joined(j, part, scores, wide):
         before = part_top[j, part, :]
         top = jnp.maximum(before, jnp.max(scores, axis=1, keepdims=True))
-        weights = jnp.exp2((scores - top[:, :1]) * factor).astype(jnp.bfloat16)
+        spread_top = jnp.concatenate([top] * (scores.shape[1] // HEAD_DIM), axis=1)
+        weights = jnp.exp2((scores - spread_top) * factor).astype(jnp.bfloat16)
         kept = jnp.exp2((before - top) * factor)
         total = jnp.dot(weights, wide, preferred_element_type=jnp.float32)
         summed = total[:, :HEAD_DIM] + kept * part_sum[j, part, :HEAD_DIM]
         weight = total[:, HEAD_DIM:] + kept * part_sum[j, part, HEAD_DIM:]
+        return top, summed, weight
+
+    def middle_finish(j, step, heads, scores, wide):
+        part = pl.ds(step * heads * rows, heads * rows)
+        top, summed, weight = joined(j, part, scores, wide)
+        part_sum[j, part, :HEAD_DIM] = summed
+        part_sum[j, part, HEAD_DIM:] = weight
+        part_top[j, part, :] = top
+
+    def tail_finish(j, step, heads, scores, wide):
+        part = pl.ds(step * heads * rows, heads * rows)
+        _, summed, weight = joined(j, part, scores, wide)
         result = (summed / weight).astype(out_ref.dtype)
         for h, c in enumerate(columns(j, step, heads)):
             out_ref[:, c] = result[h * rows:(h + 1) * rows]
 
     def stage(kind, what):
-        if kind == "relay":
+        if kind == "near":
+            from_plane(what, far - 1)
+            from_side(what, far - 2)
+        elif kind == "relay":
             from_side(what, far - 1)
             from_plane(what, far)
         elif kind == "last":
             from_side(what, far)
         elif kind == "main":
-            for j in what:
-                for d in range(far):
-                    from_core(j, d)
-                    from_core_side(j, d)
-            pipelined(what, main_pieces, MAIN_HEADS, 2, main_finish)
+            for d in range(far):
+                from_core(what, d)
+            for d in range(far - 1):
+                from_core_side(what, d)
+            pipelined((what,), main_pieces, MAIN_HEADS, MAIN_AHEAD, main_finish)
+        elif kind == "middle":
+            from_core_side(what, far - 1)
+            from_core(what, far)
+            if level > 2:
+                pipelined((what,), middle_pieces, MIDDLE_HEADS, MIDDLE_AHEAD, middle_finish)
         else:
-            for j in what:
-                from_core(j, far)
-                from_core_side(j, far)
-            pipelined(what, tail_pieces, TAIL_HEADS, 1, tail_finish)
+            from_core_side(what, far)
+            pipelined((what,), tail_pieces, TAIL_HEADS, TAIL_AHEAD, tail_finish)
 
     for j in range(KV_HEADS):
         own_copies[2 * j].wait()
@@ -257,11 +313,11 @@
     for k in range(len_buf.shape[0]):
         end = end + len_buf[k]
         start = jnp.where(end <= position, end, start)
-    key_position = (me - reach) * rows + lax.broadcasted_iota(jnp.int32, (width, rows), 0)
+    key_position = (me - reach) * rows + lax.broadcasted_iota(jnp.int32, bias.shape, 0)
     visible = (key_position >= start) & (key_position <= position)
     bias[...] = jnp.where(visible, 0.0, FILLER).astype(bias.dtype)
 
-    for d in range(1, far):
+    for d in range(1, far - 1):
         for j in range(KV_HEADS):
             from_plane(j, d)
             from_side(j, d - 1)
@@ -291,7 +347,7 @@
             scratch_shapes=[
                 pltpu.VMEM(queries.shape, queries.dtype),
                 pltpu.VMEM((KV_HEADS, 2, slots * rows, HEAD_DIM), keys.dtype),
-                pltpu.VMEM(((reach + 1) * rows, rows), keys.dtype),
+                pltpu.VMEM(((reach + 2) * rows, rows), keys.dtype),
                 pltpu.SMEM(doc_lengths.shape, doc_lengths.dtype),
                 pltpu.VMEM((KV_HEADS, GROUP * rows, 2 * HEAD_DIM), jnp.float32),
                 pltpu.VMEM((KV_HEADS, GROUP * rows, HEAD_DIM), jnp.float32),

time: 25.2 us -> 22.8 us (0.905)
  Pallas kernels: 24.1 us -> 21.6 us
    pallas_call x1, Pallas kernels: 24.1 us -> 21.6 us  [local(): pl.pallas_call(functools.partial(kernel, n, level), out_shape=jax.ShapeDt...]
where the time goes in v2:
time: 22.8 us; the launch traced here: 22.6 us
  Pallas kernels  21.6 us (95%)
  local copies, waits for them, and re-layouts  0.97 us (4%)
    pallas_call x1, Pallas kernels, local(): pl.pallas_call(functools.partial(kernel, n, level), out_shape=jax.ShapeDt...  21.6 us
    unnamed x1, local copies, waits for them, and re-layouts  0.97 us

profile of v2, /device:TPU:25, one launch (start us, length us, event | category | flops | bytes accessed | tf_op | source)
XLA Modules:
  0.0 22.6 jit_solution(14011086742112768795)
XLA Ops:
  0.0 21.6 %shard_map.46 = bf16[128,4096]{1,0:T(8,128)(2,1)S(1)} custom-call(bf16[128,4096]{1,0:T(8,128)(2,1)} %q_hbm.1, bf16[128,512]{1,0:T(8,128)(2,1)} %k_hbm.1, bf16[128,512]{1,0:T(8,128)(2,1)} %v_hbm.1, s32[16]{0:T(128)} %len_hbm.1), custom_call_target="tpu_custom_call" | custom-call | tf_op jit(solution)/shard_map/pallas_call | solution.py:342
  21.6 1.0 %copy.6 = bf16[128,4096]{1,0:T(8,128)(2,1)} copy(bf16[128,4096]{1,0:T(8,128)(2,1)S(1)} %shard_map.46) | data formatting | bytes 2097152

commit v3 on v2

--- a/solution.py
+++ b/solution.py
@@ -13,12 +13,12 @@
 HEAD_DIM = 128
 GROUP = HEADS // KV_HEADS
 FILLER = -1e30
-BY_PLANE = 1
+BY_PLANE = 2
 MAIN_HEADS = 2
-MAIN_AHEAD = 2
+MAIN_AHEAD = 0
 MIDDLE_HEADS = 2
 MIDDLE_AHEAD = 0
-TAIL_HEADS = 2
+TAIL_HEADS = 4
 TAIL_AHEAD = 0
 ORDER = (
     ("near", 0),
@@ -39,12 +39,12 @@
     ("last", 0),
     ("middle", 3),
     ("last", 1),
+    ("last", 2),
+    ("tail", 0),
     ("last", 3),
-    ("tail", 0),
-    ("last", 2),
     ("tail", 1),
+    ("tail", 2),
     ("tail", 3),
-    ("tail", 2),
 )
 
 

time: 22.8 us -> 22.7 us (level)
  no operation moved by 1% of the time
where the time goes in v3:
time: 22.7 us; the launch traced here: 22.5 us
  Pallas kernels  21.6 us (95%)
  local copies, waits for them, and re-layouts  0.97 us (4%)
    pallas_call x1, Pallas kernels, local(): pl.pallas_call(functools.partial(kernel, n, level), out_shape=jax.ShapeDt...  21.6 us
    unnamed x1, local copies, waits for them, and re-layouts  0.97 us

profile of v3, /device:TPU:25, one launch (start us, length us, event | category | flops | bytes accessed | tf_op | source)
XLA Modules:
  0.0 22.5 jit_solution(11906027536205504120)
XLA Ops:
  0.0 21.6 %shard_map.46 = bf16[128,4096]{1,0:T(8,128)(2,1)S(1)} custom-call(bf16[128,4096]{1,0:T(8,128)(2,1)} %q_hbm.1, bf16[128,512]{1,0:T(8,128)(2,1)} %k_hbm.1, bf16[128,512]{1,0:T(8,128)(2,1)} %v_hbm.1, s32[16]{0:T(128)} %len_hbm.1), custom_call_target="tpu_custom_call" | custom-call | tf_op jit(solution)/shard_map/pallas_call | solution.py:342
  21.6 1.0 %copy.6 = bf16[128,4096]{1,0:T(8,128)(2,1)} copy(bf16[128,4096]{1,0:T(8,128)(2,1)S(1)} %shard_map.46) | data formatting | bytes 2097152
